TPU v7x, 32 devices: a whole 2x2x4 slice. The times are simulated.
32 devices in a mesh: res: 8 (over z, y), ch: 4 (over x, core).
Axes of the slice: x: 2, y: 2, z: 4, core: 2. Of those that a mesh axis runs over, the one named last changes fastest.
Arguments:
- sequence_matrix: bfloat16 [8, 512, 256], P(None, 'res'), may hold values from -6 to 6
- couple_matrix: bfloat16 [32, 128, 4096], P('res', 'ch')
- block_target_entry: int32 [8, 4], P('res'), may hold values from 0 to 7, as said below
- block_present_flag: int32 [8, 4], P('res'), may hold values from 0 to 1, as said below
- amino_strand: int32 [512], P('res'), may hold values from 0 to 5, never falling along the last dimension, each value on 1 to 170 neighbouring positions
- sequence_scaling_factor: float32 [256], replicated, may hold values from 0.5 to 1.5
- query_key_value_matrix: bfloat16 [4, 256, 256], P(None, None, 'ch'), may hold values from -0.375 to 0.375
- focus_result_matrix: bfloat16 [256, 256], P('ch'), may hold values from -0.375 to 0.375
- strand_focus_offset: float32 [8], replicated, may hold values from -2 to 2
- couple_scaling_factor: float32 [128], P('ch'), may hold values from 0.5 to 1.5
- focus_offset_matrix: float32 [128, 8], P('ch')
- product_scaling_factor: float32 [256], replicated, may hold values from 0.5 to 1.5
- first_factor_matrix: bfloat16 [256, 32], replicated, may hold values from -0.375 to 0.375
- second_factor_matrix: bfloat16 [256, 32], P(None, 'ch'), may hold values from -0.375 to 0.375
- product_result_matrix: bfloat16 [128, 32, 32], P(None, None, 'ch'), may hold values from -0.8984375 to 0.8984375
- product_result_offset: float32 [128], P('ch'), may hold values from -3 to 3
Outputs:
- sequence_result_matrix: bfloat16 [8, 512, 256], P(None, 'res')
- pairwise_output: bfloat16 [32, 128, 4096], P('res', 'ch')
Inputs may be any that keep to these rules, and one draw needn't show every extreme that they name: `block_target_entry`: slot 0 of row tile r names r itself; the column tiles of one row tile are distinct. `block_present_flag`: the valid slots of each row tile are its first ones, two or more of them; in every draw some row tile has all 4 slots valid.
All inputs are finite; a program needn't handle non-finite values.
Results may differ from a plain program's by a relative error of at most 0.005.
Values may be sent and summed in bfloat16 or wider, within the bound.
No kernel may reach another device: no remote copies, remote signals or barrier semaphores. Data moves between devices by JAX's collectives and lax.ppermute only.
A program may use at most 128 MiB of HBM per device.

v0:
```python
import math
import jax
import jax.numpy as jnp
from jax import lax
from jax.sharding import PartitionSpec as P

C_Z = 128
FOCUS_NUMBER = 8
FOCUS_BREADTH = 32
PRODUCT_FEATURE = 32
EPS = 1e-05
MASKED = -1e30


def final_dimension_standardize(values, gain_vector):
    values = values.astype(jnp.float32)
    average = jnp.mean(values, axis=-1, keepdims=True)
    variance = jnp.mean(jnp.square(values - average), axis=-1, keepdims=True)
    return (values - average) * lax.rsqrt(variance + EPS) * gain_vector


def on_device(
    sequence_matrix,
    couple_matrix,
    block_target_entry,
    block_present_flag,
    amino_strand,
    sequence_scaling_factor,
    query_key_value_matrix,
    focus_result_matrix,
    strand_focus_offset,
    couple_scaling_factor,
    focus_offset_matrix,
    product_scaling_factor,
    first_factor_matrix,
    second_factor_matrix,
    product_result_matrix,
    product_result_offset,
):
    groups = lax.axis_size("ch")
    group_index = lax.axis_index("ch")
    local_heads = FOCUS_NUMBER // groups
    slot_count = couple_matrix.shape[0]
    cell_count = couple_matrix.shape[2]
    block_extent = sequence_matrix.shape[1]
    sequence_number_overall = sequence_matrix.shape[0]
    pair_field = couple_matrix.astype(jnp.float32)
    part_one = jnp.sum(pair_field, axis=1)
    part_two = jnp.sum(pair_field * pair_field, axis=1)
    sum_one, sum_two = lax.psum((part_one, part_two), "ch")
    center = sum_one / C_Z
    spread = lax.rsqrt(sum_two / C_Z - center * center + EPS)
    normed = (
        (pair_field - center[:, None, :])
        * spread[:, None, :]
        * couple_scaling_factor[None, :, None]
    )
    partial_value = jnp.einsum(
        "kcp,ch->hkp", normed, focus_offset_matrix, precision=lax.Precision.HIGHEST
    )
    head_bias = lax.psum_scatter(partial_value, "ch", scatter_dimension=0, tiled=True)
    head_bias = head_bias.astype(jnp.bfloat16)
    bias_all, cols_all, valid_all, chain_all = (
        lax.all_gather(head_bias, "res", axis=1, tiled=True),
        lax.all_gather(block_target_entry, "res", axis=0, tiled=True),
        lax.all_gather(block_present_flag, "res", axis=0, tiled=True),
        lax.all_gather(amino_strand, "res", axis=0, tiled=True),
    )
    sequence_first_layout = lax.all_to_all(
        sequence_matrix, "res", split_axis=0, concat_axis=1, tiled=True
    )
    device_rows, amino_number_here, sequence_feature_breadth = sequence_first_layout.shape
    tile_count = amino_number_here // block_extent
    sequence_standardized = final_dimension_standardize(
        sequence_first_layout, sequence_scaling_factor
    ).astype(jnp.bfloat16)
    projected_rows = jnp.einsum(
        "hbx,sxt->shbt",
        sequence_standardized,
        query_key_value_matrix,
        preferred_element_type=jnp.float32,
    ).astype(jnp.bfloat16)
    projected_rows = projected_rows.reshape(
        4, device_rows, tile_count, block_extent, local_heads, FOCUS_BREADTH
    )
    queries = projected_rows[0]
    keyset = projected_rows[1]
    valueset = projected_rows[2]
    gateset = projected_rows[3]
    chain_tiles = chain_all.reshape(tile_count, block_extent)
    bias_tiles = bias_all.reshape(local_heads, tile_count, slot_count, block_extent, block_extent)
    head_scale = lax.dynamic_slice_in_dim(
        strand_focus_offset, group_index * local_heads, local_heads, 0
    )
    block_tiles = math.gcd(tile_count, max(1, 512 // block_extent))

    def attend(block_index):
        first_tile = block_index * block_tiles
        columns = lax.dynamic_slice_in_dim(cols_all, first_tile, block_tiles, 0)
        usable = lax.dynamic_slice_in_dim(valid_all, first_tile, block_tiles, 0) > 0
        query_block = lax.dynamic_slice_in_dim(queries, first_tile, block_tiles, 1)
        key_block = keyset[:, columns]
        value_block = valueset[:, columns]
        scores = jnp.einsum(
            "rgahd,rgkbhd->rghakb", query_block, key_block, preferred_element_type=jnp.float32
        ) * FOCUS_BREADTH ** (-0.5)
        pair_part = lax.dynamic_slice_in_dim(bias_tiles, first_tile, block_tiles, 1).astype(
            jnp.float32
        )
        pair_part = pair_part.transpose(1, 0, 3, 2, 4)
        query_chain = lax.dynamic_slice_in_dim(chain_tiles, first_tile, block_tiles, 0)
        same_chain = (query_chain[:, :, None, None] == chain_tiles[columns][:, None, :, :]).astype(
            jnp.float32
        )
        scores = (
            scores
            + pair_part[None]
            + head_scale[None, None, :, None, None, None] * same_chain[None, :, None]
        )
        scores = jnp.where(usable[None, :, None, None, :, None], scores, MASKED)
        row_max = jnp.max(scores, axis=(4, 5), keepdims=True)
        exponent = jnp.exp(scores - row_max)
        attn_weights = (exponent / jnp.sum(exponent, axis=(4, 5), keepdims=True)).astype(
            jnp.bfloat16
        )
        mixed = jnp.einsum(
            "rghakb,rgkbhd->rgahd", attn_weights, value_block, preferred_element_type=jnp.float32
        )
        gate_block = lax.dynamic_slice_in_dim(gateset, first_tile, block_tiles, 1).astype(
            jnp.float32
        )
        return (mixed * jax.nn.sigmoid(gate_block)).astype(jnp.bfloat16)

    blocks = lax.map(attend, jnp.arange(tile_count // block_tiles, dtype=jnp.int32))
    attended_rows = blocks.transpose(1, 0, 2, 3, 4, 5).reshape(
        device_rows * amino_number_here, local_heads * FOCUS_BREADTH
    )
    residual_input = sequence_first_layout.reshape(
        device_rows * amino_number_here, sequence_feature_breadth
    )
    partial_out = jnp.dot(attended_rows, focus_result_matrix, preferred_element_type=jnp.float32)
    head_total = lax.psum(partial_out, "ch")
    updated_state = (
        (residual_input.astype(jnp.float32) + head_total)
        .astype(jnp.bfloat16)
        .reshape(device_rows, amino_number_here, sequence_feature_breadth)
    )
    sequence_result_matrix = lax.all_to_all(
        updated_state, "res", split_axis=1, concat_axis=0, tiled=True
    )
    outer_normed = (
        final_dimension_standardize(sequence_result_matrix, product_scaling_factor)
        .astype(jnp.bfloat16)
        .reshape(sequence_number_overall * block_extent, sequence_feature_breadth)
    )
    left_projected = (
        jnp.dot(outer_normed, first_factor_matrix, preferred_element_type=jnp.float32)
        .astype(jnp.bfloat16)
        .reshape(sequence_number_overall, block_extent * PRODUCT_FEATURE)
    )
    own_columns = block_target_entry[0]
    right_projected = (
        jnp.dot(outer_normed, second_factor_matrix, preferred_element_type=jnp.float32)
        .astype(jnp.bfloat16)
        .reshape(sequence_number_overall, block_extent, -1)
    )
    narrow = right_projected.shape[2]
    weight_flat = product_result_matrix.reshape(C_Z, PRODUCT_FEATURE * narrow)
    empty_tiles = jnp.zeros(
        (slot_count, sequence_number_overall, block_extent, narrow), jnp.bfloat16
    )
    shard_piece = lax.all_gather(right_projected, "res", axis=1, tiled=True)
    piece_rows = shard_piece.shape[1]
    offset = own_columns * block_extent
    inside = (offset >= 0) & (offset < piece_rows)

    def take_one(offset_one, inside_one, held_tile):
        taken = lax.dynamic_slice_in_dim(
            shard_piece, jnp.clip(offset_one, 0, piece_rows - block_extent), block_extent, 1
        )
        return jnp.where(inside_one, taken, held_tile)

    chosen = jax.vmap(take_one, in_axes=(0, 0, 0))(offset, inside, empty_tiles)
    left_turned = left_projected.T

    def outer_one(right_tile_rows):
        product = (
            jnp.dot(
                left_turned,
                right_tile_rows.reshape(sequence_number_overall, block_extent * narrow),
                preferred_element_type=jnp.float32,
            )
            / sequence_number_overall
        )
        product = (
            product.reshape(block_extent, PRODUCT_FEATURE, block_extent, narrow)
            .transpose(1, 3, 0, 2)
            .astype(jnp.bfloat16)
            .reshape(PRODUCT_FEATURE * narrow, cell_count)
        )
        return jnp.dot(weight_flat, product, preferred_element_type=jnp.float32)

    partials = lax.map(outer_one, chosen)
    summed = lax.psum_scatter(partials, "ch", scatter_dimension=1, tiled=True)
    keep_mask = block_present_flag[0].astype(jnp.float32)
    pairwise_output = (
        pair_field + keep_mask[:, None, None] * (summed + product_result_offset[None, :, None])
    ).astype(jnp.bfloat16)
    return (sequence_result_matrix, pairwise_output)


def solution(mesh):
    return jax.shard_map(
        on_device,
        mesh=mesh,
        in_specs=(
            P(None, "res", None),
            P("res", "ch", None),
            P("res", None),
            P("res", None),
            P("res"),
            P(),
            P(None, None, "ch"),
            P("ch", None),
            P(),
            P("ch"),
            P("ch", None),
            P(),
            P(),
            P(None, "ch"),
            P(None, None, "ch"),
            P("ch"),
        ),
        out_specs=(P(None, "res", None), P("res", "ch", None)),
        check_vma=False,
    )
```

profile of v0, /device:TPU:0, one launch (start us, length us, event | category | flops | bytes accessed | tf_op | source)
XLA Modules:
  0.0 450.4 jit_solution(9530738559762649015)
XLA Ops:
  7.2 7.5 %all-to-all-start = ((bf16[8,64,256]{2,1,0:T(8,128)(2,1)}), bf16[8,64,256]{2,1,0:T(8,128)(2,1)S(1)}, u32[]{:S(2)}, u32[]{:S(2)}) async-start(bf16[8,64,256]{2,1,0:T(8,128)(2,1)} %param.18), calls=%async_computation | async-start | bytes 524288 | tf_op jit(solution)/shard_map/all_to_all | solution.py:69
  20.0 11.8 %all-reduce = s32[512]{0:T(512)S(1)} all-reduce(s32[512]{0:T(512)S(1)} %dynamic-update-slice), channel_id=1, replica_groups=mesh['res'=8,'ch'=4] {'res'}, use_global_device_ids=true, to_apply=%add | all-reduce | flops 512 | bytes 4096
  31.9 17.9 %all-gather = s32[8,1,4]{2,1,0:T(1,128)S(1)} all-gather(s32[1,1,4]{2,1,0:T(1,128)} %bitcast.164), channel_id=1, replica_groups=mesh['res'=8,'ch'=4] {'res'}, dimensions={0}, use_global_device_ids=true | all-gather | bytes 144 | tf_op jit(solution)/shard_map/all_gather | solution.py:65
  51.9 16.8 %all-gather.1 = s32[8,1,4]{2,1,0:T(1,128)S(1)} all-gather(s32[1,1,4]{2,1,0:T(1,128)S(1)} %bitcast.165), channel_id=1, replica_groups=mesh['res'=8,'ch'=4] {'res'}, dimensions={0}, use_global_device_ids=true | all-gather | bytes 144 | tf_op jit(solution)/shard_map/all_gather | solution.py:66
  73.0 16.4 %all-reduce.10 = bf16[8,4,4096]{2,1,0:T(4,128)(2,1)S(1)} all-reduce(f32[8,4,4096]{2,1,0:T(4,128)S(1)} %copy.104), channel_id=2, replica_groups=mesh['res'=8,'ch'=4] {'ch'}, use_global_device_ids=true, to_apply=%region_6.0.clone | all-reduce | flops 131072 | bytes 786432
  89.5 31.4 %all_gather.17 = bf16[2,32,4096]{2,0,1:T(2,128)(2,1)S(1)} all-gather(bf16[2,4,4096]{2,0,1:T(2,128)(2,1)S(1)} %copy.105), channel_id=1, replica_groups=mesh['res'=8,'ch'=4] {'res'}, dimensions={1}, use_global_device_ids=true | all-gather | bytes 589824 | tf_op jit(solution)/shard_map/all_gather | solution.py:64
  136.4 31.8 %all-reduce.7.cloned.1.call-done = f32[512,256]{1,0:T(8,128)} async-done(((f32[512,256]{1,0:T(8,128)}), f32[512,256]{1,0:T(8,128)}) %all-reduce.7.cloned.1.call-update) | async-done | bytes 524304 | tf_op jit(solution)/shard_map/psum | solution.py:142
  179.1 8.0 %all-to-all-done.1 = bf16[8,2,8192]{2,1,0:T(2,128)(2,1)S(1)} async-done(((bf16[8,2,8192]{2,1,0:T(2,128)(2,1)}), bf16[8,2,8192]{2,1,0:T(2,128)(2,1)S(1)}, u32[]{:S(2)}, u32[]{:S(2)}) %all-to-all-start.1) | async-done | bytes 262176 | tf_op jit(solution)/shard_map/all_to_all | solution.py:148
  189.2 7.4 %multiply_reduce_fusion = f32[512]{0:T(512)S(1)} fusion(f32[512]{0:T(512)S(1)} %broadcast_multiply_fusion.2, bf16[512,1,256]{2,1,0:T(2,128)(2,1)S(1)} %reshape.379), kind=kLoop, calls=%fused_computation.49 | loop fusion | flops 523776 | bytes 266240 | tf_op jit(solution)/shard_map/reduce_sum | solution.py:18
  197.2 33.1 %all_gather.19 = bf16[8,512,8]{2,0,1:T(8,128)(2,1)S(1)} all-gather(bf16[8,64,8]{2,0,1:T(8,128)(2,1)S(1)} %copy.113), channel_id=1, replica_groups=mesh['res'=8,'ch'=4] {'res'}, dimensions={1}, use_global_device_ids=true | all-gather | bytes 73728 | tf_op jit(solution)/shard_map/all_gather | solution.py:172
  231.6 139.8 %while.2 = (s32[]{:T(128)}, f32[4,128,4096]{2,1,0:T(8,128)}, bf16[4,8,64,8]{3,1,2,0:T(8,128)(2,1)S(1)}, bf16[2048,8]{0,1:T(8,128)(2,1)S(1)}, bf16[128,256]{1,0:T(8,128)(2,1)S(1)}, /*index=5*/s32[]{:T(128)}) while((s32[]{:T(128)}, f32[4,128,4096]{2,1,0:T(8,128)}, bf16[4,8,64,8]{3,1,2,0:T(8,128)(2,1)S(1)}, bf16[2048,8]{0,1:T(8,128)(2,1)S(1)}, ...), condition=%wide.region_13.14_spmd, body=%wide.region_12.13_spmd.sunk | while | flops 287309824 | bytes 27418708 | solution.py:203
  232.6 8.1 %convert_element_type.203 = bf16[64,32,64,8]{1,0,3,2:T(8,128)(2,1)} reshape(bf16[2048,512]{0,1:T(8,128)(2,1)S(1)} %fusion.55) | data formatting | bytes 4194304 | tf_op jit(solution)/shard_map/while/body/eval_jaxpr/convert_element_type | solution.py:198
  240.7 14.6 %copy.154 = bf16[32,8,64,64]{3,2,1,0:T(8,128)(2,1)} copy(bf16[32,8,64,64]{0,2,1,3:T(8,128)(2,1)} %bitcast.151) | data formatting | bytes 4194304 | tf_op jit(solution)/shard_map/while/body/eval_jaxpr/convert_element_type | solution.py:198
  255.3 5.7 %reshape.383 = bf16[256,4096]{1,0:T(8,128)(2,1)S(1)} reshape(bf16[32,8,64,64]{3,2,1,0:T(8,128)(2,1)} %copy.154) | data formatting | bytes 4194304 | tf_op jit(solution)/shard_map/while/body/eval_jaxpr/reshape | solution.py:199
  267.6 8.1 %convert_element_type.203 = bf16[64,32,64,8]{1,0,3,2:T(8,128)(2,1)} reshape(bf16[2048,512]{0,1:T(8,128)(2,1)S(1)} %fusion.55) | data formatting | bytes 4194304 | tf_op jit(solution)/shard_map/while/body/eval_jaxpr/convert_element_type | solution.py:198
  275.7 14.6 %copy.154 = bf16[32,8,64,64]{3,2,1,0:T(8,128)(2,1)} copy(bf16[32,8,64,64]{0,2,1,3:T(8,128)(2,1)} %bitcast.151) | data formatting | bytes 4194304 | tf_op jit(solution)/shard_map/while/body/eval_jaxpr/convert_element_type | solution.py:198
  290.3 5.7 %reshape.383 = bf16[256,4096]{1,0:T(8,128)(2,1)S(1)} reshape(bf16[32,8,64,64]{3,2,1,0:T(8,128)(2,1)} %copy.154) | data formatting | bytes 4194304 | tf_op jit(solution)/shard_map/while/body/eval_jaxpr/reshape | solution.py:199
  302.5 8.1 %convert_element_type.203 = bf16[64,32,64,8]{1,0,3,2:T(8,128)(2,1)} reshape(bf16[2048,512]{0,1:T(8,128)(2,1)S(1)} %fusion.55) | data formatting | bytes 4194304 | tf_op jit(solution)/shard_map/while/body/eval_jaxpr/convert_element_type | solution.py:198
  310.6 14.6 %copy.154 = bf16[32,8,64,64]{3,2,1,0:T(8,128)(2,1)} copy(bf16[32,8,64,64]{0,2,1,3:T(8,128)(2,1)} %bitcast.151) | data formatting | bytes 4194304 | tf_op jit(solution)/shard_map/while/body/eval_jaxpr/convert_element_type | solution.py:198
  325.2 5.7 %reshape.383 = bf16[256,4096]{1,0:T(8,128)(2,1)S(1)} reshape(bf16[32,8,64,64]{3,2,1,0:T(8,128)(2,1)} %copy.154) | data formatting | bytes 4194304 | tf_op jit(solution)/shard_map/while/body/eval_jaxpr/reshape | solution.py:199
  337.4 8.1 %convert_element_type.203 = bf16[64,32,64,8]{1,0,3,2:T(8,128)(2,1)} reshape(bf16[2048,512]{0,1:T(8,128)(2,1)S(1)} %fusion.55) | data formatting | bytes 4194304 | tf_op jit(solution)/shard_map/while/body/eval_jaxpr/convert_element_type | solution.py:198
  345.6 14.6 %copy.154 = bf16[32,8,64,64]{3,2,1,0:T(8,128)(2,1)} copy(bf16[32,8,64,64]{0,2,1,3:T(8,128)(2,1)} %bitcast.151) | data formatting | bytes 4194304 | tf_op jit(solution)/shard_map/while/body/eval_jaxpr/convert_element_type | solution.py:198
  360.2 5.7 %reshape.383 = bf16[256,4096]{1,0:T(8,128)(2,1)S(1)} reshape(bf16[32,8,64,64]{3,2,1,0:T(8,128)(2,1)} %copy.154) | data formatting | bytes 4194304 | tf_op jit(solution)/shard_map/while/body/eval_jaxpr/reshape | solution.py:199
  372.2 68.8 %reduce-scatter.2.cloned.1.call-done = f32[4,32,4096]{2,1,0:T(8,128)} async-done(((f32[4,128,4096]{2,1,0:T(8,128)}), f32[4,32,4096]{2,1,0:T(8,128)}) %reduce-scatter.2.cloned.1.call-update) | async-done | bytes 2097168 | tf_op jit(solution)/shard_map/reduce_scatter | solution.py:204
  (149 shorter events, 70.5 us)
Async XLA Ops:
  7.2 119.0 %copy-start = (bf16[4,256,64]{1,2,0:T(8,128)(2,1)S(1)}, bf16[4,256,64]{1,2,0:T(8,128)(2,1)}, u32[]{:S(2)}) copy-start(bf16[4,256,64]{1,2,0:T(8,128)(2,1)} %param.24) | copy-start | bytes 393220
  7.2 61.8 %copy-start.17 = (u32[32]{0:T(128)S(1)}, u32[32]{0:T(128)}, u32[]{:S(2)}) copy-start(u32[32]{0:T(128)} %constant.112) | copy-start | bytes 388
  7.2 64.0 %copy-start.1 = (bf16[4,32,4096]{2,1,0:T(8,128)(2,1)S(1)}, bf16[4,32,4096]{2,1,0:T(8,128)(2,1)}, u32[]{:S(2)}) copy-start(bf16[4,32,4096]{2,1,0:T(8,128)(2,1)} %param.19) | copy-start | bytes 3145732
  7.2 44.7 %copy-start.13 = (s32[1,4]{1,0:T(1,128)S(1)}, s32[1,4]{1,0:T(1,128)}, u32[]{:S(2)}) copy-start(s32[1,4]{1,0:T(1,128)} %param.21) | copy-start | bytes 52
  7.2 61.7 %copy-start.15 = (f32[8]{0:T(128)S(1)}, f32[8]{0:T(128)}, u32[]{:S(2)}) copy-start(f32[8]{0:T(128)} %param.26) | copy-start | bytes 100
  7.2 64.0 %copy-start.16 = (f32[32]{0:T(128)S(1)}, f32[32]{0:T(128)}, u32[]{:S(2)}) copy-start(f32[32]{0:T(128)} %param.27) | copy-start | bytes 388
  7.2 64.0 %copy-start.14 = (f32[32,8]{0,1:T(8,128)S(1)}, f32[32,8]{0,1:T(8,128)}, u32[]{:S(2)}) copy-start(f32[32,8]{0,1:T(8,128)} %param.28) | copy-start | bytes 3076
  7.2 118.2 %all-to-all-start = ((bf16[8,64,256]{2,1,0:T(8,128)(2,1)}), bf16[8,64,256]{2,1,0:T(8,128)(2,1)S(1)}, u32[]{:S(2)}, u32[]{:S(2)}) async-start(bf16[8,64,256]{2,1,0:T(8,128)(2,1)} %param.18), calls=%async_computation | async-start | bytes 524288 | tf_op jit(solution)/shard_map/all_to_all | solution.py:69
  14.7 55.5 %all-reduce.9.cloned.1.call-start = ((), (), s32[]{:S(2)}) async-start(), calls=%async_computation.5 | async-start | bytes 262144 | tf_op jit(solution)/shard_map/psum | solution.py:50
  17.1 151.0 %all-reduce.7.cloned.1.call-start = ((), (), s32[]{:S(2)}) async-start(), calls=%async_computation.3 | async-start | bytes 1048576 | tf_op jit(solution)/shard_map/psum | solution.py:142
  123.5 2.5 copy-start.9
  133.4 1.0 copy-start.3
  133.4 1.1 copy-start.4
  134.5 0.8 copy-start.6
  136.3 42.6 %copy-start.5 = (bf16[128,32,8]{0,2,1:T(8,128)(2,1)S(1)}, bf16[128,32,8]{0,2,1:T(8,128)(2,1)}, u32[]{:S(2)}) copy-start(bf16[128,32,8]{0,2,1:T(8,128)(2,1)} %param.32) | copy-start | bytes 196612
  136.3 42.7 %copy-start.12 = (s32[1,4]{1,0:T(1,128)S(1)}, s32[1,4]{1,0:T(1,128)}, u32[]{:S(2)}) copy-start(s32[1,4]{1,0:T(1,128)} %param.20) | copy-start | bytes 52
  172.4 24.2 %copy-start.10 = (f32[256]{0:T(256)S(1)}, f32[256]{0:T(256)}, u32[]{:S(2)}) copy-start(f32[256]{0:T(256)} %param.29) | copy-start | bytes 3076
  173.2 23.6 %copy-start.8 = (bf16[256,8]{0,1:T(8,128)(2,1)S(1)}, bf16[256,8]{0,1:T(8,128)(2,1)}, u32[]{:S(2)}) copy-start(bf16[256,8]{0,1:T(8,128)(2,1)} %param.31) | copy-start | bytes 12292
  173.2 13.9 %all-to-all-start.1 = ((bf16[8,2,8192]{2,1,0:T(2,128)(2,1)}), bf16[8,2,8192]{2,1,0:T(2,128)(2,1)S(1)}, u32[]{:S(2)}, u32[]{:S(2)}) async-start(bf16[8,2,8192]{2,1,0:T(2,128)(2,1)} %reshape.378), calls=%async_computation.1 | async-start | bytes 524288 | tf_op jit(solution)/shard_map/all_to_all | solution.py:148
  178.8 262.1 %reduce-scatter.2.cloned.1.call-start = ((), (), s32[]{:S(2)}) async-start(), calls=%async_computation.4 | async-start | bytes 10485760 | tf_op jit(solution)/shard_map/reduce_scatter | solution.py:204
  187.3 43.0 %copy-start.7 = (bf16[256,32]{0,1:T(8,128)(2,1)S(1)}, bf16[256,32]{0,1:T(8,128)(2,1)}, u32[]{:S(2)}) copy-start(bf16[256,32]{0,1:T(8,128)(2,1)} %param.30) | copy-start | bytes 49156
  371.4 69.5 %copy-start.2 = (bf16[4,32,4096]{2,1,0:T(8,128)(2,1)S(1)}, bf16[4,32,4096]{2,1,0:T(8,128)(2,1)}, u32[]{:S(2)}) copy-start(bf16[4,32,4096]{2,1,0:T(8,128)(2,1)} %param.19) | copy-start | bytes 3145732
  371.4 69.5 %copy-start.11 = (f32[32]{0:T(128)S(1)}, f32[32]{0:T(128)}, u32[]{:S(2)}) copy-start(f32[32]{0:T(128)} %param.33) | copy-start | bytes 388
Sparse Core Ops, SparseCore 0:
  18.5 33.1 all-reduce.8
  136.5 31.6 all-reduce.6
  371.6 69.3 reduce-scatter.1
where the time goes:
time: 452 us; the launch traced here: 450 us
  local copies, waits for them, and re-layouts  146 us (32%)
  blocking collectives  127 us (28%)
  waiting for transfers between devices  109 us (24%)
  other arithmetic  21.8 us (5%)
  matrix products  17.3 us (4%)
  between operations  15.5 us (3%)
  starting transfers between devices  13.2 us (3%)
    convert_element_type x8, local copies, waits for them, and re-layouts, outer_one(): product = product.reshape(block_extent, PRODUCT_FEATURE, block_extent, na...  90.9 us
    reduce_scatter x1, waiting for transfers between devices, on_device(): summed = lax.psum_scatter(partials, 'ch', scatter_dimension=1, tiled=True)  68.8 us
    all_gather x1, blocking collectives, on_device(): shard_piece = lax.all_gather(right_projected, 'res', axis=1, tiled=True)  33.1 us
    psum x1, waiting for transfers between devices, on_device(): head_total = lax.psum(partial_out, 'ch')  31.8 us
    all_gather x1, blocking collectives, on_device(): lax.all_gather(head_bias, 'res', axis=1, tiled=True)  31.4 us
    unnamed x2, blocking collectives  28.2 us
    reshape x4, local copies, waits for them, and re-layouts, outer_one(): product = product.reshape(block_extent, PRODUCT_FEATURE, block_extent, na...  22.7 us
    all_gather x1, blocking collectives, on_device(): lax.all_gather(block_target_entry, 'res', axis=0, tiled=True)  17.9 us
  transfers between devices with their start and end apart: 5, of which 3 were waited for; matrix products, arithmetic and copies ran while one was open for 4% of the time, Pallas kernels for 0%

commit v1 on v0

--- a/solution.py
+++ b/solution.py
@@ -10,6 +10,16 @@
 PRODUCT_FEATURE = 32
 EPS = 1e-05
 MASKED = -1e30
+
+
+def local_data_handle(buf, across="ch"):
+    n = lax.axis_size(across)
+    z, far_arr = (buf, 0)
+    while 1 << far_arr < n:
+        passed = lax.ppermute(z, axis_name=across, perm=[(h, h ^ 1 << far_arr) for h in range(n)])
+        z = z + passed
+        far_arr = far_arr + 1
+    return z
 
 
 def final_dimension_standardize(values, gain_vector):
@@ -139,7 +149,7 @@
         device_rows * amino_number_here, sequence_feature_breadth
     )
     partial_out = jnp.dot(attended_rows, focus_result_matrix, preferred_element_type=jnp.float32)
-    head_total = lax.psum(partial_out, "ch")
+    head_total = local_data_handle(partial_out)
     updated_state = (
         (residual_input.astype(jnp.float32) + head_total)
         .astype(jnp.bfloat16)

time: 452 us -> 434 us (0.960)
  waiting for transfers between devices: 109 us -> 91.8 us
    psum x1 -> x0, waiting for transfers between devices: 31.8 us -> none  [on_device(): head_total = lax.psum(partial_out, 'ch')]
    ppermute x0 -> x2, waiting for transfers between devices: none -> 14.2 us  [local_data_handle(): lax.ppermute(z, axis_name=across, perm=[(h, h ^ 1 << far_arr) for h in ra...]
  transfers between devices with their start and end apart: 5 -> 6, of which waited for: 3 -> 4; matrix products, arithmetic and copies ran while one was open for 4% -> 4% of each run, Pallas kernels for 0% -> 0%
where the time goes in v1:
time: 434 us; the launch traced here: 432 us
  local copies, waits for them, and re-layouts  146 us (34%)
  blocking collectives  128 us (29%)
  waiting for transfers between devices  91.8 us (21%)
  other arithmetic  20.9 us (5%)
  matrix products  16.5 us (4%)
  between operations  15.8 us (4%)
  starting transfers between devices  13.1 us (3%)
    convert_element_type x8, local copies, waits for them, and re-layouts, outer_one(): product = product.reshape(block_extent, PRODUCT_FEATURE, block_extent, na...  90.9 us
    reduce_scatter x1, waiting for transfers between devices, on_device(): summed = lax.psum_scatter(partials, 'ch', scatter_dimension=1, tiled=True)  69.3 us
    all_gather x1, blocking collectives, on_device(): shard_piece = lax.all_gather(right_projected, 'res', axis=1, tiled=True)  33.2 us
    all_gather x1, blocking collectives, on_device(): lax.all_gather(head_bias, 'res', axis=1, tiled=True)  31.6 us
    unnamed x2, blocking collectives  28.2 us
    reshape x4, local copies, waits for them, and re-layouts, outer_one(): product = product.reshape(block_extent, PRODUCT_FEATURE, block_extent, na...  22.7 us
    all_gather x1, blocking collectives, on_device(): lax.all_gather(block_target_entry, 'res', axis=0, tiled=True)  17.9 us
    all_gather x1, blocking collectives, on_device(): lax.all_gather(block_present_flag, 'res', axis=0, tiled=True)  16.8 us
  transfers between devices with their start and end apart: 6, of which 4 were waited for; matrix products, arithmetic and copies ran while one was open for 4% of the time, Pallas kernels for 0%

profile of v1, /device:TPU:0, one launch (start us, length us, event | category | flops | bytes accessed | tf_op | source)
XLA Modules:
  0.0 432.3 jit_solution(13230358237185332678)
XLA Ops:
  7.2 7.5 %all-to-all-start = ((bf16[8,64,256]{2,1,0:T(8,128)(2,1)}), bf16[8,64,256]{2,1,0:T(8,128)(2,1)S(1)}, u32[]{:S(2)}, u32[]{:S(2)}) async-start(bf16[8,64,256]{2,1,0:T(8,128)(2,1)} %param.18), calls=%async_computation | async-start | bytes 524288 | tf_op jit(solution)/shard_map/all_to_all | solution.py:79
  19.9 11.8 %all-reduce = s32[512]{0:T(512)S(1)} all-reduce(s32[512]{0:T(512)S(1)} %dynamic-update-slice), channel_id=1, replica_groups=mesh['res'=8,'ch'=4] {'res'}, use_global_device_ids=true, to_apply=%add | all-reduce | flops 512 | bytes 4096
  31.8 17.9 %all-gather = s32[8,1,4]{2,1,0:T(1,128)S(1)} all-gather(s32[1,1,4]{2,1,0:T(1,128)} %bitcast.164), channel_id=1, replica_groups=mesh['res'=8,'ch'=4] {'res'}, dimensions={0}, use_global_device_ids=true | all-gather | bytes 144 | tf_op jit(solution)/shard_map/all_gather | solution.py:75
  51.9 16.8 %all-gather.1 = s32[8,1,4]{2,1,0:T(1,128)S(1)} all-gather(s32[1,1,4]{2,1,0:T(1,128)S(1)} %bitcast.165), channel_id=1, replica_groups=mesh['res'=8,'ch'=4] {'res'}, dimensions={0}, use_global_device_ids=true | all-gather | bytes 144 | tf_op jit(solution)/shard_map/all_gather | solution.py:76
  73.0 16.4 %all-reduce.7 = bf16[8,4,4096]{2,1,0:T(4,128)(2,1)S(1)} all-reduce(f32[8,4,4096]{2,1,0:T(4,128)S(1)} %copy.104), channel_id=2, replica_groups=mesh['res'=8,'ch'=4] {'ch'}, use_global_device_ids=true, to_apply=%region_6.0.clone | all-reduce | flops 131072 | bytes 786432
  89.5 31.6 %all_gather.17 = bf16[2,32,4096]{2,0,1:T(2,128)(2,1)S(1)} all-gather(bf16[2,4,4096]{2,0,1:T(2,128)(2,1)S(1)} %copy.105), channel_id=1, replica_groups=mesh['res'=8,'ch'=4] {'res'}, dimensions={1}, use_global_device_ids=true | all-gather | bytes 589824 | tf_op jit(solution)/shard_map/all_gather | solution.py:74
  139.4 12.3 %collective-permute-done.1 = f32[512,256]{1,0:T(8,128)S(1)} collective-permute-done((f32[512,256]{1,0:T(8,128)S(1)}, f32[512,256]{1,0:T(8,128)S(1)}, u32[]{:S(2)}, u32[]{:S(2)}) %collective-permute-start.1) | collective-permute-done | bytes 524320 | tf_op jit(solution)/shard_map/ppermute | solution.py:19
  159.8 8.1 %all-to-all-done.1 = bf16[8,2,8192]{2,1,0:T(2,128)(2,1)S(1)} async-done(((bf16[8,2,8192]{2,1,0:T(2,128)(2,1)}), bf16[8,2,8192]{2,1,0:T(2,128)(2,1)S(1)}, u32[]{:S(2)}, u32[]{:S(2)}) %all-to-all-start.1) | async-done | bytes 262176 | tf_op jit(solution)/shard_map/all_to_all | solution.py:158
  170.0 7.4 %multiply_reduce_fusion = f32[512]{0:T(512)S(1)} fusion(f32[512]{0:T(512)S(1)} %broadcast_multiply_fusion.2, bf16[512,1,256]{2,1,0:T(2,128)(2,1)S(1)} %reshape.379), kind=kLoop, calls=%fused_computation.49 | loop fusion | flops 523776 | bytes 266240 | tf_op jit(solution)/shard_map/reduce_sum | solution.py:28
  178.1 33.2 %all_gather.19 = bf16[8,512,8]{2,0,1:T(8,128)(2,1)S(1)} all-gather(bf16[8,64,8]{2,0,1:T(8,128)(2,1)S(1)} %copy.113), channel_id=1, replica_groups=mesh['res'=8,'ch'=4] {'res'}, dimensions={1}, use_global_device_ids=true | all-gather | bytes 73728 | tf_op jit(solution)/shard_map/all_gather | solution.py:182
  212.5 139.8 %while.2 = (s32[]{:T(128)}, f32[4,128,4096]{2,1,0:T(8,128)}, bf16[4,8,64,8]{3,1,2,0:T(8,128)(2,1)S(1)}, bf16[2048,8]{0,1:T(8,128)(2,1)S(1)}, bf16[128,256]{1,0:T(8,128)(2,1)S(1)}, /*index=5*/s32[]{:T(128)}) while((s32[]{:T(128)}, f32[4,128,4096]{2,1,0:T(8,128)}, bf16[4,8,64,8]{3,1,2,0:T(8,128)(2,1)S(1)}, bf16[2048,8]{0,1:T(8,128)(2,1)S(1)}, ...), condition=%wide.region_12.13_spmd, body=%wide.region_11.12_spmd.sunk | while | flops 287309824 | bytes 27418708 | solution.py:213
  213.6 8.1 %convert_element_type.203 = bf16[64,32,64,8]{1,0,3,2:T(8,128)(2,1)} reshape(bf16[2048,512]{0,1:T(8,128)(2,1)S(1)} %fusion.55) | data formatting | bytes 4194304 | tf_op jit(solution)/shard_map/while/body/eval_jaxpr/convert_element_type | solution.py:208
  221.7 14.6 %copy.154 = bf16[32,8,64,64]{3,2,1,0:T(8,128)(2,1)} copy(bf16[32,8,64,64]{0,2,1,3:T(8,128)(2,1)} %bitcast.151) | data formatting | bytes 4194304 | tf_op jit(solution)/shard_map/while/body/eval_jaxpr/convert_element_type | solution.py:208
  236.3 5.7 %reshape.383 = bf16[256,4096]{1,0:T(8,128)(2,1)S(1)} reshape(bf16[32,8,64,64]{3,2,1,0:T(8,128)(2,1)} %copy.154) | data formatting | bytes 4194304 | tf_op jit(solution)/shard_map/while/body/eval_jaxpr/reshape | solution.py:209
  248.5 8.1 %convert_element_type.203 = bf16[64,32,64,8]{1,0,3,2:T(8,128)(2,1)} reshape(bf16[2048,512]{0,1:T(8,128)(2,1)S(1)} %fusion.55) | data formatting | bytes 4194304 | tf_op jit(solution)/shard_map/while/body/eval_jaxpr/convert_element_type | solution.py:208
  256.7 14.6 %copy.154 = bf16[32,8,64,64]{3,2,1,0:T(8,128)(2,1)} copy(bf16[32,8,64,64]{0,2,1,3:T(8,128)(2,1)} %bitcast.151) | data formatting | bytes 4194304 | tf_op jit(solution)/shard_map/while/body/eval_jaxpr/convert_element_type | solution.py:208
  271.3 5.7 %reshape.383 = bf16[256,4096]{1,0:T(8,128)(2,1)S(1)} reshape(bf16[32,8,64,64]{3,2,1,0:T(8,128)(2,1)} %copy.154) | data formatting | bytes 4194304 | tf_op jit(solution)/shard_map/while/body/eval_jaxpr/reshape | solution.py:209
  283.5 8.1 %convert_element_type.203 = bf16[64,32,64,8]{1,0,3,2:T(8,128)(2,1)} reshape(bf16[2048,512]{0,1:T(8,128)(2,1)S(1)} %fusion.55) | data formatting | bytes 4194304 | tf_op jit(solution)/shard_map/while/body/eval_jaxpr/convert_element_type | solution.py:208
  291.6 14.6 %copy.154 = bf16[32,8,64,64]{3,2,1,0:T(8,128)(2,1)} copy(bf16[32,8,64,64]{0,2,1,3:T(8,128)(2,1)} %bitcast.151) | data formatting | bytes 4194304 | tf_op jit(solution)/shard_map/while/body/eval_jaxpr/convert_element_type | solution.py:208
  306.2 5.7 %reshape.383 = bf16[256,4096]{1,0:T(8,128)(2,1)S(1)} reshape(bf16[32,8,64,64]{3,2,1,0:T(8,128)(2,1)} %copy.154) | data formatting | bytes 4194304 | tf_op jit(solution)/shard_map/while/body/eval_jaxpr/reshape | solution.py:209
  318.4 8.1 %convert_element_type.203 = bf16[64,32,64,8]{1,0,3,2:T(8,128)(2,1)} reshape(bf16[2048,512]{0,1:T(8,128)(2,1)S(1)} %fusion.55) | data formatting | bytes 4194304 | tf_op jit(solution)/shard_map/while/body/eval_jaxpr/convert_element_type | solution.py:208
  326.5 14.6 %copy.154 = bf16[32,8,64,64]{3,2,1,0:T(8,128)(2,1)} copy(bf16[32,8,64,64]{0,2,1,3:T(8,128)(2,1)} %bitcast.151) | data formatting | bytes 4194304 | tf_op jit(solution)/shard_map/while/body/eval_jaxpr/convert_element_type | solution.py:208
  341.1 5.7 %reshape.383 = bf16[256,4096]{1,0:T(8,128)(2,1)S(1)} reshape(bf16[32,8,64,64]{3,2,1,0:T(8,128)(2,1)} %copy.154) | data formatting | bytes 4194304 | tf_op jit(solution)/shard_map/while/body/eval_jaxpr/reshape | solution.py:209
  353.2 69.3 %reduce-scatter.2.cloned.1.call-done = f32[4,32,4096]{2,1,0:T(8,128)} async-done(((f32[4,128,4096]{2,1,0:T(8,128)}), f32[4,32,4096]{2,1,0:T(8,128)}) %reduce-scatter.2.cloned.1.call-update) | async-done | bytes 2097168 | tf_op jit(solution)/shard_map/reduce_scatter | solution.py:214
  (151 shorter events, 70.5 us)
Async XLA Ops:
  7.2 119.1 %copy-start = (bf16[4,256,64]{1,2,0:T(8,128)(2,1)S(1)}, bf16[4,256,64]{1,2,0:T(8,128)(2,1)}, u32[]{:S(2)}) copy-start(bf16[4,256,64]{1,2,0:T(8,128)(2,1)} %param.24) | copy-start | bytes 393220
  7.2 61.7 %copy-start.17 = (u32[32]{0:T(128)S(1)}, u32[32]{0:T(128)}, u32[]{:S(2)}) copy-start(u32[32]{0:T(128)} %constant.112) | copy-start | bytes 388
  7.2 63.9 %copy-start.1 = (bf16[4,32,4096]{2,1,0:T(8,128)(2,1)S(1)}, bf16[4,32,4096]{2,1,0:T(8,128)(2,1)}, u32[]{:S(2)}) copy-start(bf16[4,32,4096]{2,1,0:T(8,128)(2,1)} %param.19) | copy-start | bytes 3145732
  7.2 44.7 %copy-start.13 = (s32[1,4]{1,0:T(1,128)S(1)}, s32[1,4]{1,0:T(1,128)}, u32[]{:S(2)}) copy-start(s32[1,4]{1,0:T(1,128)} %param.21) | copy-start | bytes 52
  7.2 61.6 %copy-start.15 = (f32[8]{0:T(128)S(1)}, f32[8]{0:T(128)}, u32[]{:S(2)}) copy-start(f32[8]{0:T(128)} %param.26) | copy-start | bytes 100
  7.2 63.9 %copy-start.16 = (f32[32]{0:T(128)S(1)}, f32[32]{0:T(128)}, u32[]{:S(2)}) copy-start(f32[32]{0:T(128)} %param.27) | copy-start | bytes 388
  7.2 63.9 %copy-start.14 = (f32[32,8]{0,1:T(8,128)S(1)}, f32[32,8]{0,1:T(8,128)}, u32[]{:S(2)}) copy-start(f32[32,8]{0,1:T(8,128)} %param.28) | copy-start | bytes 3076
  7.2 118.3 %all-to-all-start = ((bf16[8,64,256]{2,1,0:T(8,128)(2,1)}), bf16[8,64,256]{2,1,0:T(8,128)(2,1)S(1)}, u32[]{:S(2)}, u32[]{:S(2)}) async-start(bf16[8,64,256]{2,1,0:T(8,128)(2,1)} %param.18), calls=%async_computation | async-start | bytes 524288 | tf_op jit(solution)/shard_map/all_to_all | solution.py:79
  14.7 55.5 %all-reduce.6.cloned.1.call-start = ((), (), s32[]{:S(2)}) async-start(), calls=%async_computation.4 | async-start | bytes 262144 | tf_op jit(solution)/shard_map/psum | solution.py:60
  123.6 2.5 copy-start.9
  133.5 1.0 copy-start.3
  133.5 1.1 copy-start.4
  134.6 0.8 copy-start.6
  135.7 2.0 collective-permute-start
  137.7 21.9 %copy-start.5 = (bf16[128,32,8]{0,2,1:T(8,128)(2,1)S(1)}, bf16[128,32,8]{0,2,1:T(8,128)(2,1)}, u32[]{:S(2)}) copy-start(bf16[128,32,8]{0,2,1:T(8,128)(2,1)} %param.32) | copy-start | bytes 196612
  137.7 22.0 %copy-start.12 = (s32[1,4]{1,0:T(1,128)S(1)}, s32[1,4]{1,0:T(1,128)}, u32[]{:S(2)}) copy-start(s32[1,4]{1,0:T(1,128)} %param.20) | copy-start | bytes 52
  137.7 14.0 %collective-permute-start.1 = (f32[512,256]{1,0:T(8,128)S(1)}, f32[512,256]{1,0:T(8,128)S(1)}, u32[]{:S(2)}, u32[]{:S(2)}) collective-permute-start(f32[512,256]{1,0:T(8,128)S(1)} %add.120), channel_id=1, source_target_pairs={{0,2},{1,3},{2,0},{3,1},{4,6},{5,7},{6,4},{7,5},{8,10},{9,11},{10,... | collective-permute-start | bytes 1572872 | tf_op jit(solution)/shard_map/ppermute | solution.py:19
  155.0 22.4 %copy-start.10 = (f32[256]{0:T(256)S(1)}, f32[256]{0:T(256)}, u32[]{:S(2)}) copy-start(f32[256]{0:T(256)} %param.29) | copy-start | bytes 3076
  155.8 21.9 %copy-start.8 = (bf16[256,8]{0,1:T(8,128)(2,1)S(1)}, bf16[256,8]{0,1:T(8,128)(2,1)}, u32[]{:S(2)}) copy-start(bf16[256,8]{0,1:T(8,128)(2,1)} %param.31) | copy-start | bytes 12292
  155.8 12.1 %all-to-all-start.1 = ((bf16[8,2,8192]{2,1,0:T(2,128)(2,1)}), bf16[8,2,8192]{2,1,0:T(2,128)(2,1)S(1)}, u32[]{:S(2)}, u32[]{:S(2)}) async-start(bf16[8,2,8192]{2,1,0:T(2,128)(2,1)} %reshape.378), calls=%async_computation.1 | async-start | bytes 524288 | tf_op jit(solution)/shard_map/all_to_all | solution.py:158
  159.4 263.2 %reduce-scatter.2.cloned.1.call-start = ((), (), s32[]{:S(2)}) async-start(), calls=%async_computation.3 | async-start | bytes 10485760 | tf_op jit(solution)/shard_map/reduce_scatter | solution.py:214
  168.2 43.1 %copy-start.7 = (bf16[256,32]{0,1:T(8,128)(2,1)S(1)}, bf16[256,32]{0,1:T(8,128)(2,1)}, u32[]{:S(2)}) copy-start(bf16[256,32]{0,1:T(8,128)(2,1)} %param.30) | copy-start | bytes 49156
  352.4 70.1 %copy-start.2 = (bf16[4,32,4096]{2,1,0:T(8,128)(2,1)S(1)}, bf16[4,32,4096]{2,1,0:T(8,128)(2,1)}, u32[]{:S(2)}) copy-start(bf16[4,32,4096]{2,1,0:T(8,128)(2,1)} %param.19) | copy-start | bytes 3145732
  352.4 70.1 %copy-start.11 = (f32[32]{0:T(128)S(1)}, f32[32]{0:T(128)}, u32[]{:S(2)}) copy-start(f32[32]{0:T(128)} %param.33) | copy-start | bytes 388
Sparse Core Ops, SparseCore 0:
  18.5 33.1 all-reduce.5
  352.5 69.9 reduce-scatter.1
